TPU v7x, 1024 devices: a whole 4x8x16 slice. The times are simulated.
1024 devices in a mesh: dp: 8 (over y), node: 16 (over z), local: 8 (over x, core).
Axes of the slice: x: 4, y: 8, z: 16, core: 2. Of those that a mesh axis runs over, the one named last changes fastest.
Arguments:
- tokens: bfloat16 [16384, 2048], P(('dp', 'node', 'local')), parts along dimension 0, may hold values from -6 to 6
- cotangent: bfloat16 [16384, 2048], P(('dp', 'node', 'local')), parts along dimension 0, may hold values from -6 to 6
- expert_ids: int32 [16384, 8], P(('dp', 'node', 'local')), parts along dimension 0, may hold values from 0 to 127, all different within a row; in each aligned block of 16 rows (0 to 15, 16 to 31, ...) at most 2 rows name the same one
- combine: float32 [16384, 8], P(('dp', 'node', 'local')), parts along dimension 0, may hold values from 0.05 to 0.3
- w_gate_up: bfloat16 [128, 2048, 768], P(('node', 'local')), may hold values from -0.125 to 0.125
- w_down: bfloat16 [128, 384, 2048], P(('node', 'local')), may hold values from -0.3125 to 0.3125
Outputs:
- mixed: bfloat16 [16384, 2048], P(('dp', 'node', 'local')), parts along dimension 0
- grad_tokens: bfloat16 [16384, 2048], P(('dp', 'node', 'local')), parts along dimension 0
- grad_combine: float32 [16384, 8], P(('dp', 'node', 'local')), parts along dimension 0
There are 8 independent parts, one for each index of `dp`. A program takes and returns all parts, laid end to end along the dimension named above; an argument that names none is the same for every part. Nothing has to cross between parts.
Inputs may be any that keep to these rules, and one draw needn't show every extreme that they name: `expert_ids`: each row names 8 different experts. Among the rows of one device no expert is named more than 2 times, a bound that some block reaches.
All inputs are finite; a program needn't handle non-finite values.
Results may differ from a plain program's by a relative error of at most 0.012.
Values may be sent and summed in bfloat16 or wider, within the bound.
No kernel may reach another device: no remote copies, remote signals or barrier semaphores. Data moves between devices by JAX's collectives and lax.ppermute only.
A program may use at most 32 MiB of HBM per device.

v0:
```python
import jax
import jax.numpy as jnp
from jax import lax
from jax.sharding import PartitionSpec as P


def expert_forward(rows, w_gate_up, w_down):
    width = w_down.shape[0]
    projected = jnp.dot(rows, w_gate_up, preferred_element_type=jnp.float32)
    gate = projected[:, :width]
    upward = projected[:, width:]
    hidden = (gate * jax.nn.sigmoid(gate) * upward).astype(jnp.bfloat16)
    output = jnp.dot(hidden, w_down, preferred_element_type=jnp.float32).astype(jnp.bfloat16)
    return (output, gate, upward)


def expert_backward(grads, gate, upward, w_gate_up, w_down):
    grad_hidden = lax.dot_general(
        grads, w_down, (((1,), (1,)), ((), ())), preferred_element_type=jnp.float32
    )
    sigmoid = jax.nn.sigmoid(gate)
    grad_gate = grad_hidden * upward * sigmoid * (1.0 + gate * (1.0 - sigmoid))
    grad_up = grad_hidden * gate * sigmoid
    paired = jnp.concatenate([grad_gate, grad_up], axis=1).astype(jnp.bfloat16)
    back = lax.dot_general(
        paired, w_gate_up, (((1,), (1,)), ((), ())), preferred_element_type=jnp.float32
    )
    return back.astype(jnp.bfloat16)


def slot_tables(expert_ids, combine, experts, capacity):
    tok_rows, top_count = expert_ids.shape
    flat_ids = expert_ids.reshape(-1)
    onehot = (flat_ids[:, None] == jnp.arange(experts, dtype=jnp.int32)[None, :]).astype(jnp.int32)
    before = jnp.cumsum(onehot, axis=0) - onehot
    ranks = jnp.sum(before * onehot, axis=1)
    slots = (flat_ids * capacity + ranks).reshape(tok_rows, top_count)
    matches = slots[None, :, :] == jnp.arange(experts * capacity, dtype=jnp.int32)[:, None, None]
    placing = jnp.any(matches, axis=2).astype(jnp.bfloat16)
    slot_weight = jnp.sum(jnp.where(matches, combine[None, :, :], 0.0), axis=(1, 2))
    return (slots, placing, slot_weight)


def per_device(tokens, cotangent, expert_ids, combine, w_gate_up, w_down):
    node_count = lax.axis_size("node")
    local_count = lax.axis_size("local")
    experts = node_count * local_count
    tok_rows, top_count = expert_ids.shape
    width = tokens.shape[1]
    capacity = max(2, 2 * tok_rows * top_count // experts)
    gate_up_one = w_gate_up[0]
    down_one = w_down[0]
    slots, placing, slot_weight = slot_tables(expert_ids, combine, experts, capacity)
    send_x = jnp.dot(placing, tokens, preferred_element_type=jnp.float32).astype(jnp.bfloat16)
    send_x = send_x.reshape(node_count, local_count, capacity, width)
    send_g = jnp.dot(placing, cotangent, preferred_element_type=jnp.float32) * slot_weight[:, None]
    send_g = send_g.astype(jnp.bfloat16).reshape(node_count, local_count, capacity, width)
    arrived = lax.all_to_all(
        lax.all_to_all(send_x, "node", split_axis=0, concat_axis=0, tiled=True),
        "local",
        split_axis=1,
        concat_axis=1,
        tiled=True,
    )
    output, gate, upward = expert_forward(arrived.reshape(-1, width), gate_up_one, down_one)
    output = output.reshape(node_count, local_count, capacity, width)
    came_back = lax.all_to_all(
        lax.all_to_all(output, "node", split_axis=0, concat_axis=0, tiled=True),
        "local",
        split_axis=1,
        concat_axis=1,
        tiled=True,
    )
    grad_rows = lax.all_to_all(
        lax.all_to_all(send_g, "node", split_axis=0, concat_axis=0, tiled=True),
        "local",
        split_axis=1,
        concat_axis=1,
        tiled=True,
    )
    back = expert_backward(grad_rows.reshape(-1, width), gate, upward, gate_up_one, down_one)
    back = back.reshape(node_count, local_count, capacity, width)
    back_home = lax.all_to_all(
        lax.all_to_all(back, "node", split_axis=0, concat_axis=0, tiled=True),
        "local",
        split_axis=1,
        concat_axis=1,
        tiled=True,
    )
    picked = jnp.take(came_back.reshape(-1, width), slots, axis=0).astype(jnp.float32)
    picked_back = jnp.take(back_home.reshape(-1, width), slots, axis=0).astype(jnp.float32)
    mixed = jnp.sum(combine[:, :, None] * picked, axis=1).astype(jnp.bfloat16)
    grad_tokens = jnp.sum(picked_back, axis=1).astype(jnp.bfloat16)
    grad_combine = jnp.sum(picked * cotangent.astype(jnp.float32)[:, None, :], axis=2)
    return (mixed, grad_tokens, grad_combine)


def solution(mesh):
    placed = (
        P(("dp", "node", "local"), None),
        P(("dp", "node", "local"), None),
        P(("dp", "node", "local"), None),
        P(("dp", "node", "local"), None),
        P(("node", "local"), None, None),
        P(("node", "local"), None, None),
    )
    return jax.shard_map(
        per_device,
        mesh=mesh,
        in_specs=placed,
        out_specs=(
            P(("dp", "node", "local"), None),
            P(("dp", "node", "local"), None),
            P(("dp", "node", "local"), None),
        ),
        check_vma=False,
    )
```

profile of v0, /device:TPU:1, one launch (start us, length us, event | category | flops | bytes accessed | tf_op | source)
XLA Modules:
  0.0 348.9 jit_solution(36604559548816991)
XLA Ops:
  7.2 19.5 %all-to-all-start = ((bf16[16,8,2,2048]{3,2,1,0:T(2,128)(2,1)}), bf16[16,8,2,2048]{3,2,1,0:T(2,128)(2,1)}, u32[]{:S(2)}, u32[]{:S(2)}) async-start(bf16[16,8,2,2048]{3,2,1,0:T(2,128)(2,1)} %reshape.49), calls=%async_computation | async-start | bytes 2097152 | tf_op jit(solution)/shard_map/all_to_all | solution.py:59
  30.8 40.9 %all-to-all-done = bf16[16,8,2,2048]{3,2,1,0:T(2,128)(2,1)} async-done(((bf16[16,8,2,2048]{3,2,1,0:T(2,128)(2,1)}), bf16[16,8,2,2048]{3,2,1,0:T(2,128)(2,1)}, u32[]{:S(2)}, u32[]{:S(2)}) %all-to-all-start) | async-done | bytes 1048608 | tf_op jit(solution)/shard_map/all_to_all | solution.py:59
  71.7 13.1 %all-to-all-start.4 = ((bf16[16,8,2,2048]{3,2,1,0:T(2,128)(2,1)}), bf16[16,8,2,2048]{3,2,1,0:T(2,128)(2,1)}, u32[]{:S(2)}, u32[]{:S(2)}) async-start(bf16[16,8,2,2048]{3,2,1,0:T(2,128)(2,1)} %reshape.53), calls=%async_computation.4 | async-start | bytes 2097152 | tf_op jit(solution)/shard_map/all_to_all | solution.py:75
  84.8 3.1 copy.57
  87.8 42.3 %all-to-all-done.4 = bf16[16,8,2,2048]{3,2,1,0:T(2,128)(2,1)} async-done(((bf16[16,8,2,2048]{3,2,1,0:T(2,128)(2,1)}), bf16[16,8,2,2048]{3,2,1,0:T(2,128)(2,1)}, u32[]{:S(2)}, u32[]{:S(2)}) %all-to-all-start.4) | async-done | bytes 1048608 | tf_op jit(solution)/shard_map/all_to_all | solution.py:75
  130.1 9.9 %all-to-all-start.1 = ((bf16[16,8,2,2048]{3,2,0,1:T(2,128)(2,1)}), bf16[16,8,2,2048]{3,2,0,1:T(2,128)(2,1)}, u32[]{:S(2)}, u32[]{:S(2)}) async-start(bf16[16,8,2,2048]{3,2,0,1:T(2,128)(2,1)} %copy.57), calls=%async_computation.1 | async-start | bytes 2097152 | tf_op jit(solution)/shard_map/all_to_all | solution.py:58
  143.1 12.0 %all-to-all-done.1 = bf16[16,8,2,2048]{3,2,0,1:T(2,128)(2,1)} async-done(((bf16[16,8,2,2048]{3,2,0,1:T(2,128)(2,1)}), bf16[16,8,2,2048]{3,2,0,1:T(2,128)(2,1)}, u32[]{:S(2)}, u32[]{:S(2)}) %all-to-all-start.1) | async-done | bytes 1048608 | tf_op jit(solution)/shard_map/all_to_all | solution.py:58
  155.1 5.1 %all-to-all-start.5 = ((bf16[16,8,2,2048]{3,2,0,1:T(2,128)(2,1)}), bf16[16,8,2,2048]{3,2,0,1:T(2,128)(2,1)}, u32[]{:S(2)}, u32[]{:S(2)}) async-start(bf16[16,8,2,2048]{3,2,0,1:T(2,128)(2,1)} %copy.62), calls=%async_computation.5 | async-start | bytes 2097152 | tf_op jit(solution)/shard_map/all_to_all | solution.py:74
  160.2 3.2 copy.58
  175.3 7.7 %all-to-all-start.2 = ((bf16[16,8,2,2048]{3,2,1,0:T(2,128)(2,1)}), bf16[16,8,2,2048]{3,2,1,0:T(2,128)(2,1)}, u32[]{:S(2)}, u32[]{:S(2)}) async-start(bf16[16,8,2,2048]{3,2,1,0:T(2,128)(2,1)} %reshape.51), calls=%async_computation.2 | async-start | bytes 2097152 | tf_op jit(solution)/shard_map/all_to_all | solution.py:68
  183.0 3.2 copy.63
  195.6 32.0 %all-to-all-done.2 = bf16[16,8,2,2048]{3,2,1,0:T(2,128)(2,1)} async-done(((bf16[16,8,2,2048]{3,2,1,0:T(2,128)(2,1)}), bf16[16,8,2,2048]{3,2,1,0:T(2,128)(2,1)}, u32[]{:S(2)}, u32[]{:S(2)}) %all-to-all-start.2) | async-done | bytes 1048608 | tf_op jit(solution)/shard_map/all_to_all | solution.py:68
  227.6 13.5 %all-to-all-start.6 = ((bf16[16,8,2,2048]{3,2,1,0:T(2,128)(2,1)}), bf16[16,8,2,2048]{3,2,1,0:T(2,128)(2,1)}, u32[]{:S(2)}, u32[]{:S(2)}) async-start(bf16[16,8,2,2048]{3,2,1,0:T(2,128)(2,1)} %reshape.55), calls=%async_computation.6 | async-start | bytes 2097152 | tf_op jit(solution)/shard_map/all_to_all | solution.py:84
  241.1 3.1 copy.59
  244.2 42.3 %all-to-all-done.6 = bf16[16,8,2,2048]{3,2,1,0:T(2,128)(2,1)} async-done(((bf16[16,8,2,2048]{3,2,1,0:T(2,128)(2,1)}), bf16[16,8,2,2048]{3,2,1,0:T(2,128)(2,1)}, u32[]{:S(2)}, u32[]{:S(2)}) %all-to-all-start.6) | async-done | bytes 1048608 | tf_op jit(solution)/shard_map/all_to_all | solution.py:84
  286.5 9.7 %all-to-all-start.3 = ((bf16[16,8,2,2048]{3,2,0,1:T(2,128)(2,1)}), bf16[16,8,2,2048]{3,2,0,1:T(2,128)(2,1)}, u32[]{:S(2)}, u32[]{:S(2)}) async-start(bf16[16,8,2,2048]{3,2,0,1:T(2,128)(2,1)} %copy.59), calls=%async_computation.3 | async-start | bytes 2097152 | tf_op jit(solution)/shard_map/all_to_all | solution.py:67
  296.2 3.1 copy.64
  299.3 12.0 %all-to-all-done.3 = bf16[16,8,2,2048]{3,2,0,1:T(2,128)(2,1)} async-done(((bf16[16,8,2,2048]{3,2,0,1:T(2,128)(2,1)}), bf16[16,8,2,2048]{3,2,0,1:T(2,128)(2,1)}, u32[]{:S(2)}, u32[]{:S(2)}) %all-to-all-start.3) | async-done | bytes 1048608 | tf_op jit(solution)/shard_map/all_to_all | solution.py:67
  311.3 5.1 %all-to-all-start.7 = ((bf16[16,8,2,2048]{3,2,0,1:T(2,128)(2,1)}), bf16[16,8,2,2048]{3,2,0,1:T(2,128)(2,1)}, u32[]{:S(2)}, u32[]{:S(2)}) async-start(bf16[16,8,2,2048]{3,2,0,1:T(2,128)(2,1)} %copy.64), calls=%async_computation.7 | async-start | bytes 2097152 | tf_op jit(solution)/shard_map/all_to_all | solution.py:83
  316.5 3.2 copy.60
  321.9 9.6 %all-to-all-done.7 = bf16[16,8,2,2048]{3,2,0,1:T(2,128)(2,1)} async-done(((bf16[16,8,2,2048]{3,2,0,1:T(2,128)(2,1)}), bf16[16,8,2,2048]{3,2,0,1:T(2,128)(2,1)}, u32[]{:S(2)}, u32[]{:S(2)}) %all-to-all-start.7) | async-done | bytes 1048608 | tf_op jit(solution)/shard_map/all_to_all | solution.py:83
  331.5 3.2 copy.65
  336.9 3.6 %gather_fusion = bf16[128,2048]{1,0:T(8,128)(2,1)} fusion(bf16[256,2048]{1,0:T(8,128)(2,1)} %reshape.52, s32[1024]{0:T(1024)S(1)} %pad_clamp_fusion), kind=kCustom, calls=%fused_computation.clone | custom fusion | bytes 1049088 | tf_op jit(solution)/shard_map/jit(_take)/gather | solution.py:90
  340.5 3.6 %gather_fusion.1 = bf16[128,2048]{1,0:T(8,128)(2,1)} fusion(bf16[256,2048]{1,0:T(8,128)(2,1)} %reshape.56, s32[1024]{0:T(1024)S(1)} %pad_clamp_fusion), kind=kCustom, calls=%fused_computation.1.clone | custom fusion | bytes 1049088 | tf_op jit(solution)/shard_map/jit(_take)/gather | solution.py:91
  (43 shorter events, 44.6 us)
Async XLA Ops:
  0.6 165.0 %copy-start = (bf16[1,2048,768]{2,1,0:T(8,128)(2,1)S(1)}, bf16[1,2048,768]{2,1,0:T(8,128)(2,1)}, u32[]{:S(2)}) copy-start(bf16[1,2048,768]{2,1,0:T(8,128)(2,1)} %param.12) | copy-start | bytes 9437188
  4.6 22.0 %copy-start.2 = (f32[16,8]{0,1:T(8,128)S(1)}, f32[16,8]{0,1:T(8,128)}, u32[]{:S(2)}) copy-start(f32[16,8]{0,1:T(8,128)} %param.11) | copy-start | bytes 1540
  4.6 22.2 %copy-start.1 = (bf16[16,2048]{1,0:T(8,128)(2,1)S(1)}, bf16[16,2048]{1,0:T(8,128)(2,1)}, u32[]{:S(2)}) copy-start(bf16[16,2048]{1,0:T(8,128)(2,1)} %param.9) | copy-start | bytes 196612
  7.2 64.5 %all-to-all-start = ((bf16[16,8,2,2048]{3,2,1,0:T(2,128)(2,1)}), bf16[16,8,2,2048]{3,2,1,0:T(2,128)(2,1)}, u32[]{:S(2)}, u32[]{:S(2)}) async-start(bf16[16,8,2,2048]{3,2,1,0:T(2,128)(2,1)} %reshape.49), calls=%async_computation | async-start | bytes 2097152 | tf_op jit(solution)/shard_map/all_to_all | solution.py:59
  71.7 58.4 %all-to-all-start.4 = ((bf16[16,8,2,2048]{3,2,1,0:T(2,128)(2,1)}), bf16[16,8,2,2048]{3,2,1,0:T(2,128)(2,1)}, u32[]{:S(2)}, u32[]{:S(2)}) async-start(bf16[16,8,2,2048]{3,2,1,0:T(2,128)(2,1)} %reshape.53), calls=%async_computation.4 | async-start | bytes 2097152 | tf_op jit(solution)/shard_map/all_to_all | solution.py:75
  130.1 25.0 %all-to-all-start.1 = ((bf16[16,8,2,2048]{3,2,0,1:T(2,128)(2,1)}), bf16[16,8,2,2048]{3,2,0,1:T(2,128)(2,1)}, u32[]{:S(2)}, u32[]{:S(2)}) async-start(bf16[16,8,2,2048]{3,2,0,1:T(2,128)(2,1)} %copy.57), calls=%async_computation.1 | async-start | bytes 2097152 | tf_op jit(solution)/shard_map/all_to_all | solution.py:58
  155.1 20.2 %all-to-all-start.5 = ((bf16[16,8,2,2048]{3,2,0,1:T(2,128)(2,1)}), bf16[16,8,2,2048]{3,2,0,1:T(2,128)(2,1)}, u32[]{:S(2)}, u32[]{:S(2)}) async-start(bf16[16,8,2,2048]{3,2,0,1:T(2,128)(2,1)} %copy.62), calls=%async_computation.5 | async-start | bytes 2097152 | tf_op jit(solution)/shard_map/all_to_all | solution.py:74
  165.6 3.2 copy-start.3
  167.9 0.9 copy-start.4
  175.3 52.4 %all-to-all-start.2 = ((bf16[16,8,2,2048]{3,2,1,0:T(2,128)(2,1)}), bf16[16,8,2,2048]{3,2,1,0:T(2,128)(2,1)}, u32[]{:S(2)}, u32[]{:S(2)}) async-start(bf16[16,8,2,2048]{3,2,1,0:T(2,128)(2,1)} %reshape.51), calls=%async_computation.2 | async-start | bytes 2097152 | tf_op jit(solution)/shard_map/all_to_all | solution.py:68
  227.6 58.8 %all-to-all-start.6 = ((bf16[16,8,2,2048]{3,2,1,0:T(2,128)(2,1)}), bf16[16,8,2,2048]{3,2,1,0:T(2,128)(2,1)}, u32[]{:S(2)}, u32[]{:S(2)}) async-start(bf16[16,8,2,2048]{3,2,1,0:T(2,128)(2,1)} %reshape.55), calls=%async_computation.6 | async-start | bytes 2097152 | tf_op jit(solution)/shard_map/all_to_all | solution.py:84
  286.5 24.8 %all-to-all-start.3 = ((bf16[16,8,2,2048]{3,2,0,1:T(2,128)(2,1)}), bf16[16,8,2,2048]{3,2,0,1:T(2,128)(2,1)}, u32[]{:S(2)}, u32[]{:S(2)}) async-start(bf16[16,8,2,2048]{3,2,0,1:T(2,128)(2,1)} %copy.59), calls=%async_computation.3 | async-start | bytes 2097152 | tf_op jit(solution)/shard_map/all_to_all | solution.py:67
  311.3 20.2 %all-to-all-start.7 = ((bf16[16,8,2,2048]{3,2,0,1:T(2,128)(2,1)}), bf16[16,8,2,2048]{3,2,0,1:T(2,128)(2,1)}, u32[]{:S(2)}, u32[]{:S(2)}) async-start(bf16[16,8,2,2048]{3,2,0,1:T(2,128)(2,1)} %copy.64), calls=%async_computation.7 | async-start | bytes 2097152 | tf_op jit(solution)/shard_map/all_to_all | solution.py:83
where the time goes:
time: 350 us; the launch traced here: 349 us
  waiting for transfers between devices  193 us (55%)
  starting transfers between devices  83.5 us (24%)
  local copies, waits for them, and re-layouts  54.1 us (15%)
  matrix products  12.5 us (4%)
  other arithmetic  4.92 us (1%)
    all_to_all x1, waiting for transfers between devices, per_device(): lax.all_to_all(send_g, 'node', split_axis=0, concat_axis=0, tiled=True)  42.3 us
    all_to_all x1, waiting for transfers between devices, per_device(): lax.all_to_all(back, 'node', split_axis=0, concat_axis=0, tiled=True)  42.3 us
    all_to_all x1, waiting for transfers between devices, per_device(): lax.all_to_all(send_x, 'node', split_axis=0, concat_axis=0, tiled=True)  40.9 us
    all_to_all x1, waiting for transfers between devices, per_device(): lax.all_to_all(output, 'node', split_axis=0, concat_axis=0, tiled=True)  32 us
    all_to_all x1, starting transfers between devices, per_device(): lax.all_to_all(send_x, 'node', split_axis=0, concat_axis=0, tiled=True)  19.5 us
    all_to_all x1, starting transfers between devices, per_device(): lax.all_to_all(back, 'node', split_axis=0, concat_axis=0, tiled=True)  13.5 us
    all_to_all x1, starting transfers between devices, per_device(): lax.all_to_all(send_g, 'node', split_axis=0, concat_axis=0, tiled=True)  13.1 us
    all_to_all x1, waiting for transfers between devices, per_device(): lax.all_to_all(lax.all_to_all(send_x, 'node', split_axis=0, concat_axis=0...  12 us
  transfers between devices with their start and end apart: 8, of which 8 were waited for; matrix products, arithmetic and copies ran while one was open for 13% of the time, Pallas kernels for 0%

commit v1 on v0

v1 whole, which is shorter than its diff:
```python
import jax
import jax.numpy as jnp
from jax import lax
from jax.experimental import pallas as pl
from jax.experimental.pallas import tpu as pltpu
from jax.sharding import PartitionSpec as P

EXTRA = 128
F32 = jnp.float32
BF16 = jnp.bfloat16


def split3(value):
    hi = value.astype(BF16)
    rest = value - hi.astype(F32)
    mid = rest.astype(BF16)
    low = (rest - mid.astype(F32)).astype(BF16)
    return hi, mid, low


def dot(a, b):
    return jnp.dot(a, b, preferred_element_type=F32)


def dispatch_kernel(dims, node_ref, all_ref, send_ref, place_ref, hi_ref, mid_ref):
    blocks, rows, peers, cap, top, width = dims
    tokens = blocks * rows
    slots = peers * blocks * cap
    per_peer = blocks * cap
    extra = all_ref[:, 2 * width :].astype(F32)
    base = (node_ref[0] * peers).astype(F32)
    slot = lax.broadcasted_iota(jnp.int32, (tokens, slots), 1)
    wanted = (slot // per_peer).astype(F32) + base
    has = jnp.zeros((tokens, slots), F32)
    weight = jnp.zeros((tokens, slots), F32)
    for k in range(top):
        match = extra[:, k : k + 1] == wanted
        value = (
            extra[:, top + k : top + k + 1]
            + extra[:, 2 * top + k : 2 * top + k + 1]
            + extra[:, 3 * top + k : 3 * top + k + 1]
        )
        has = jnp.where(match, 1.0, has)
        weight = jnp.where(match, value, weight)
    row = lax.broadcasted_iota(jnp.int32, (tokens, tokens), 0)
    col = lax.broadcasted_iota(jnp.int32, (tokens, tokens), 1)
    earlier = jnp.where((row // rows == col // rows) & (col < row), 1.0, 0.0).astype(BF16)
    rank = dot(earlier, has.astype(BF16))
    block = (lax.broadcasted_iota(jnp.int32, (tokens, slots), 0) // rows * cap).astype(F32)
    place = jnp.where((has > 0.0) & (block + rank == (slot % per_peer).astype(F32)), 1.0, 0.0)
    weight = place * weight
    place_bf = place.astype(BF16)
    hi, mid, low = split3(weight)
    place_ref[...] = place_bf
    hi_ref[...] = hi
    mid_ref[...] = mid
    over_tokens = (((0,), (0,)), ((), ()))
    ones = jnp.ones((tokens, 128), BF16)
    slot_weight = (
        lax.dot_general(hi, ones, over_tokens, preferred_element_type=F32)
        + lax.dot_general(mid, ones, over_tokens, preferred_element_type=F32)
        + lax.dot_general(low, ones, over_tokens, preferred_element_type=F32)
    )[:, :1]
    send_ref[:, :width] = lax.dot_general(
        place_bf, all_ref[:, :width], over_tokens, preferred_element_type=F32
    ).astype(BF16)
    picked = lax.dot_general(
        place_bf, all_ref[:, width : 2 * width], over_tokens, preferred_element_type=F32
    )
    send_ref[:, width:] = (picked * slot_weight).astype(BF16)


def expert_kernel(width, rows_ref, gate_up_ref, down_ref, out_ref):
    hidden_width = down_ref.shape[0]
    projected = dot(rows_ref[:, :width], gate_up_ref[...])
    gate = projected[:, :hidden_width]
    upward = projected[:, hidden_width:]
    sigmoid = jax.nn.sigmoid(gate)
    hidden = (gate * sigmoid * upward).astype(BF16)
    out_ref[:, :width] = dot(hidden, down_ref[...]).astype(BF16)
    over_last = (((1,), (1,)), ((), ()))
    grad_hidden = lax.dot_general(
        rows_ref[:, width:], down_ref[...], over_last, preferred_element_type=F32
    )
    grad_gate = grad_hidden * upward * sigmoid * (1.0 + gate * (1.0 - sigmoid))
    grad_up = grad_hidden * gate * sigmoid
    paired = jnp.concatenate([grad_gate.astype(BF16), grad_up.astype(BF16)], axis=1)
    out_ref[:, width:] = lax.dot_general(
        paired, gate_up_ref[...], over_last, preferred_element_type=F32
    ).astype(BF16)


def combine_kernel(dims, node_ref, all_ref, rows_ref, place_ref, hi_ref, mid_ref, sum_ref):
    blocks, rows, peers, cap, top, width = dims
    tokens = blocks * rows
    slots = peers * blocks * cap
    output = rows_ref[:, :width]
    sum_ref[:, :width] = (dot(hi_ref[...], output) + dot(mid_ref[...], output)).astype(BF16)
    sum_ref[:, width : 2 * width] = dot(place_ref[...], rows_ref[:, width:]).astype(BF16)
    over_last = (((1,), (1,)), ((), ()))
    against = lax.dot_general(
        all_ref[:, width : 2 * width], output, over_last, preferred_element_type=F32
    )
    kept = against * place_ref[...].astype(F32)
    peer_of = lax.broadcasted_iota(jnp.int32, (slots, EXTRA), 0) // (blocks * cap)
    lane_of = lax.broadcasted_iota(jnp.int32, (slots, EXTRA), 1)
    fold = jnp.where(peer_of == lane_of, 1.0, 0.0).astype(BF16)
    hi, mid, low = split3(kept)
    by_peer = dot(hi, fold) + dot(mid, fold) + dot(low, fold)
    ids = all_ref[:, 2 * width :].astype(F32)
    base = (node_ref[0] * peers).astype(F32)
    lane = lax.broadcasted_iota(jnp.int32, (tokens, EXTRA), 1)
    chosen = jnp.zeros((tokens, EXTRA), F32)
    for p in range(peers):
        chosen = jnp.where(ids == base + p, by_peer[:, p : p + 1], chosen)
    chosen = jnp.where(lane < top, chosen, 0.0)
    hi, mid, low = split3(chosen)
    sum_ref[:, 2 * width :] = (
        hi.astype(F32)
        + pltpu.roll(mid.astype(F32), top, 1)
        + pltpu.roll(low.astype(F32), 2 * top, 1)
    ).astype(BF16)


def per_device(tokens, cotangent, expert_ids, combine, w_gate_up, w_down):
    blocks = lax.axis_size("node")
    peers = lax.axis_size("local")
    rows, top = expert_ids.shape
    width = tokens.shape[1]
    cap = 2
    dims = (blocks, rows, peers, cap, top, width)
    slots = peers * blocks * cap
    count = blocks * rows
    node = lax.axis_index("node").astype(jnp.int32).reshape(1)
    hi = lax.reduce_precision(combine, 8, 7)
    mid = lax.reduce_precision(combine - hi, 8, 7)
    low = combine - hi - mid
    pieces = (hi.astype(BF16), mid.astype(BF16), low.astype(BF16))
    packed = jnp.concatenate(
        [
            tokens,
            cotangent,
            expert_ids.astype(BF16),
            *pieces,
            jnp.zeros((rows, EXTRA - 4 * top), BF16),
        ],
        axis=1,
    )
    gathered = lax.all_gather(packed, "node", axis=0, tiled=True)
    smem = pl.BlockSpec(memory_space=pltpu.SMEM)
    vmem = pl.BlockSpec(memory_space=pltpu.VMEM)
    send, place, hi, mid = pl.pallas_call(
        lambda *refs: dispatch_kernel(dims, *refs),
        out_shape=(
            jax.ShapeDtypeStruct((slots, 2 * width), BF16),
            jax.ShapeDtypeStruct((count, slots), BF16),
            jax.ShapeDtypeStruct((count, slots), BF16),
            jax.ShapeDtypeStruct((count, slots), BF16),
        ),
        in_specs=[smem, vmem],
        out_specs=(vmem,) * 4,
        name="dispatch",
    )(node, gathered)
    arrived = lax.all_to_all(
        send.reshape(peers, blocks * cap, 2 * width), "local", 0, 0, tiled=True
    )
    worked = pl.pallas_call(
        lambda *refs: expert_kernel(width, *refs),
        out_shape=jax.ShapeDtypeStruct((slots, 2 * width), BF16),
        in_specs=[vmem] * 3,
        out_specs=vmem,
        name="expert",
    )(arrived.reshape(slots, 2 * width), w_gate_up[0], w_down[0])
    returned = lax.all_to_all(
        worked.reshape(peers, blocks * cap, 2 * width), "local", 0, 0, tiled=True
    )
    partial = pl.pallas_call(
        lambda *refs: combine_kernel(dims, *refs),
        out_shape=jax.ShapeDtypeStruct((count, 2 * width + EXTRA), BF16),
        in_specs=[smem] + [vmem] * 5,
        out_specs=vmem,
        name="combine",
    )(node, gathered, returned.reshape(slots, 2 * width), place, hi, mid)
    summed = lax.psum_scatter(partial, "node", scatter_dimension=0, tiled=True)
    last = summed[:, 2 * width :].astype(F32)
    grad_combine = last[:, :top] + last[:, top : 2 * top] + last[:, 2 * top : 3 * top]
    return summed[:, :width], summed[:, width : 2 * width], grad_combine


def solution(mesh):
    rows = P(("dp", "node", "local"), None)
    experts = P(("node", "local"), None, None)
    return jax.shard_map(
        per_device,
        mesh=mesh,
        in_specs=(rows, rows, rows, rows, experts, experts),
        out_specs=(rows, rows, rows),
        check_vma=False,
    )
```

time: 350 us -> 261 us (0.75)
  the two profiles are of different devices: /device:TPU:1 before, /device:TPU:4 now
where the time goes in v1:
time: 261 us; the launch traced here: 260 us
  waiting for transfers between devices  160 us (61%)
  blocking collectives  60.8 us (23%)
  Pallas kernels  18.3 us (7%)
  between operations  14 us (5%)
  local copies, waits for them, and re-layouts  4.72 us (2%)
    all_gather x1, waiting for transfers between devices, per_device(): gathered = lax.all_gather(packed, 'node', axis=0, tiled=True)  84.7 us
    reduce_scatter x1, waiting for transfers between devices, per_device(): summed = lax.psum_scatter(partial, 'node', scatter_dimension=0, tiled=True)  75.4 us
    all_to_all x1, blocking collectives, per_device(): lax.all_to_all(worked.reshape(peers, blocks * cap, 2 * width), 'local', 0...  31.5 us
    all_to_all x1, blocking collectives, per_device(): lax.all_to_all(send.reshape(peers, blocks * cap, 2 * width), 'local', 0,...  29.2 us
    pallas_call x1, Pallas kernels, per_device(): pl.pallas_call(lambda *refs: expert_kernel(width, *refs), out_shape=jax.S...  7.85 us
    pallas_call x1, Pallas kernels, per_device(): pl.pallas_call(lambda *refs: combine_kernel(dims, *refs), out_shape=jax.S...  5.69 us
  transfers between devices with their start and end apart: 2, of which 2 were waited for; matrix products, arithmetic and copies ran while one was open for 0% of the time, Pallas kernels for 0%

profile of v1, /device:TPU:4, one launch (start us, length us, event | category | flops | bytes accessed | tf_op | source)
XLA Modules:
  0.0 260.2 jit_solution(4324193375199634909)
XLA Ops:
  7.2 0.0 all-gather.2.cloned.1.call-start
  7.2 0.7 reduce_precision.6
  7.9 0.8 copy.14
  8.7 0.7 convert_element_type.15
  9.3 0.1 copy.16
  9.4 0.1 copy.13
  9.5 1.6 concatenate.3
  11.1 0.0 all-gather.2.cloned.1.call-update
  11.2 0.0 reduce-scatter.2.cloned.1.call-start
  11.2 84.7 %all-gather.2.cloned.1.call-done.refs_1_ = bf16[256,4224]{1,0:T(8,128)(2,1)} async-done(((bf16[16,4224]{1,0:T(8,128)(2,1)}), bf16[256,4224]{1,0:T(8,128)(2,1)}) %all-gather.2.cloned.1.call-update) | async-done | bytes 2162704 | tf_op jit(solution)/shard_map/all_gather | solution.py:149
  95.9 4.7 %dispatch.1 = (bf16[256,4096]{1,0:T(8,128)(2,1)}, bf16[256,256]{1,0:T(8,128)(2,1)}, bf16[256,256]{1,0:T(8,128)(2,1)}, bf16[256,256]{1,0:T(8,128)(2,1)}) custom-call(s32[1]{0:T(128)} %bitcast.refs_0_, bf16[256,4224]{1,0:T(8,128)(2,1)} %all-gather.2.cloned.1.call-done.refs_1_), custom_call_target="tpu_custom_call" | custom-call | tf_op jit(solution)/shard_map/dispatch/pallas_call | solution.py:152
  100.7 29.2 %all_to_all.10 = bf16[8,32,4096]{2,1,0:T(8,128)(2,1)} all-to-all(bf16[8,32,4096]{2,1,0:T(8,128)(2,1)} %bitcast.11), channel_id=1, replica_groups=mesh['dp'=8,'node'=16,'local'=8] {'local'}, dimensions={0} | all-to-all | bytes 4194304 | tf_op jit(solution)/shard_map/all_to_all | solution.py:164
  129.9 7.8 %expert.1 = bf16[256,4096]{1,0:T(8,128)(2,1)} custom-call(bf16[256,4096]{1,0:T(8,128)(2,1)} %bitcast.7, bf16[2048,768]{1,0:T(8,128)(2,1)} %bitcast.10, bf16[384,2048]{1,0:T(8,128)(2,1)} %bitcast.12), custom_call_target="tpu_custom_call" | custom-call | tf_op jit(solution)/shard_map/expert/pallas_call | solution.py:167
  137.8 31.5 %all_to_all.11 = bf16[8,32,4096]{2,1,0:T(8,128)(2,1)} all-to-all(bf16[8,32,4096]{2,1,0:T(8,128)(2,1)} %bitcast.8), channel_id=1, replica_groups=mesh['dp'=8,'node'=16,'local'=8] {'local'}, dimensions={0} | all-to-all | bytes 4194304 | tf_op jit(solution)/shard_map/all_to_all | solution.py:174
  169.3 5.7 %combine.1 = bf16[256,4224]{1,0:T(8,128)(2,1)} custom-call(s32[1]{0:T(128)} %bitcast.refs_0_, bf16[256,4224]{1,0:T(8,128)(2,1)} %all-gather.2.cloned.1.call-done.refs_1_, bf16[256,4096]{1,0:T(8,128)(2,1)} %bitcast.9, bf16[256,256]{1,0:T(8,128)(2,1)} %get-tuple-element.8.refs_3_, bf16[256,256]{1,0:T(8,128)(2,1)} %get-tuple-element.9.refs_4_, ...), custom_call_target="tpu_custom_call" | custom-call | tf_op jit(solution)/shard_map/combine/pallas_call | solution.py:177
  175.0 0.0 reduce-scatter.2.cloned.1.call-update
  175.0 75.4 %reduce-scatter.2.cloned.1.call-done = bf16[16,4224]{1,0:T(8,128)(2,1)} async-done(((bf16[256,4224]{1,0:T(8,128)(2,1)}), bf16[16,4224]{1,0:T(8,128)(2,1)}) %reduce-scatter.2.cloned.1.call-update) | async-done | bytes 135184 | tf_op jit(solution)/shard_map/reduce_scatter | solution.py:184
  250.4 0.7 slice_convert_fusion
  251.1 0.1 slice_add_fusion
  251.2 0.7 copy.17
  251.9 1.5 fusion.1
  (2 shorter events, 0.0 us)
Async XLA Ops:
  7.2 88.8 %all-gather.2.cloned.1.call-start = ((), (), s32[]{:S(2)}) async-start(), calls=%async_computation.3 | async-start | bytes 2297856 | tf_op jit(solution)/shard_map/all_gather | solution.py:149
  11.2 239.3 %reduce-scatter.2.cloned.1.call-start = ((), (), s32[]{:S(2)}) async-start(), calls=%async_computation.4 | async-start | bytes 2297856 | tf_op jit(solution)/shard_map/reduce_scatter | solution.py:184
Sparse Core Ops, SparseCore 0:
  11.3 84.6 all-gather.1
  175.2 75.2 reduce-scatter.1

commit v2 on v1

--- a/solution.py
+++ b/solution.py
@@ -6,6 +6,7 @@
 from jax.sharding import PartitionSpec as P
 
 EXTRA = 128
+PAIR = 2
 F32 = jnp.float32
 BF16 = jnp.bfloat16
 
@@ -123,15 +124,19 @@
 
 
 def per_device(tokens, cotangent, expert_ids, combine, w_gate_up, w_down):
-    blocks = lax.axis_size("node")
-    peers = lax.axis_size("local")
+    nodes = lax.axis_size("node")
+    locals_ = lax.axis_size("local")
+    blocks = nodes // PAIR
+    peers = PAIR * locals_
+    rings = [list(range(first, nodes, PAIR)) for first in range(PAIR)]
+    pairs = [list(range(q * peers, (q + 1) * peers)) for q in range(blocks)]
     rows, top = expert_ids.shape
     width = tokens.shape[1]
     cap = 2
     dims = (blocks, rows, peers, cap, top, width)
     slots = peers * blocks * cap
     count = blocks * rows
-    node = lax.axis_index("node").astype(jnp.int32).reshape(1)
+    node = (lax.axis_index("node") // PAIR).astype(jnp.int32).reshape(1)
     hi = lax.reduce_precision(combine, 8, 7)
     mid = lax.reduce_precision(combine - hi, 8, 7)
     low = combine - hi - mid
@@ -146,7 +151,7 @@
         ],
         axis=1,
     )
-    gathered = lax.all_gather(packed, "node", axis=0, tiled=True)
+    gathered = lax.all_gather(packed, "node", axis_index_groups=rings, axis=0, tiled=True)
     smem = pl.BlockSpec(memory_space=pltpu.SMEM)
     vmem = pl.BlockSpec(memory_space=pltpu.VMEM)
     send, place, hi, mid = pl.pallas_call(
@@ -161,9 +166,18 @@
         out_specs=(vmem,) * 4,
         name="dispatch",
     )(node, gathered)
-    arrived = lax.all_to_all(
-        send.reshape(peers, blocks * cap, 2 * width), "local", 0, 0, tiled=True
-    )
+
+    def exchange(value):
+        return lax.all_to_all(
+            value.reshape(peers, blocks * cap, 2 * width),
+            ("node", "local"),
+            0,
+            0,
+            axis_index_groups=pairs,
+            tiled=True,
+        )
+
+    arrived = exchange(send)
     worked = pl.pallas_call(
         lambda *refs: expert_kernel(width, *refs),
         out_shape=jax.ShapeDtypeStruct((slots, 2 * width), BF16),
@@ -171,9 +185,7 @@
         out_specs=vmem,
         name="expert",
     )(arrived.reshape(slots, 2 * width), w_gate_up[0], w_down[0])
-    returned = lax.all_to_all(
-        worked.reshape(peers, blocks * cap, 2 * width), "local", 0, 0, tiled=True
-    )
+    returned = exchange(worked)
     partial = pl.pallas_call(
         lambda *refs: combine_kernel(dims, *refs),
         out_shape=jax.ShapeDtypeStruct((count, 2 * width + EXTRA), BF16),
@@ -181,7 +193,9 @@
         out_specs=vmem,
         name="combine",
     )(node, gathered, returned.reshape(slots, 2 * width), place, hi, mid)
-    summed = lax.psum_scatter(partial, "node", scatter_dimension=0, tiled=True)
+    summed = lax.psum_scatter(
+        partial, "node", scatter_dimension=0, axis_index_groups=rings, tiled=True
+    )
     last = summed[:, 2 * width :].astype(F32)
     grad_combine = last[:, :top] + last[:, top : 2 * top] + last[:, 2 * top : 3 * top]
     return summed[:, :width], summed[:, width : 2 * width], grad_combine

time: 261 us -> 219 us (0.84)
  the two profiles are of different devices: /device:TPU:4 before, /device:TPU:1 now
where the time goes in v2:
time: 219 us; the launch traced here: 216 us
  waiting for transfers between devices  111 us (51%)
  blocking collectives  67.2 us (31%)
  Pallas kernels  16.3 us (7%)
  between operations  14.1 us (6%)
  local copies, waits for them, and re-layouts  4.71 us (2%)
    all_to_all x2, blocking collectives, exchange(): lax.all_to_all(value.reshape(peers, blocks * cap, 2 * width), ('node', 'l...  67.2 us
    all_gather x1, waiting for transfers between devices, per_device(): lax.all_gather(packed, 'node', axis_index_groups=rings, axis=0, tiled=True)  62.4 us
    reduce_scatter x1, waiting for transfers between devices, per_device(): lax.psum_scatter(partial, 'node', scatter_dimension=0, axis_index_groups=...  48.9 us
    pallas_call x1, Pallas kernels, per_device(): pl.pallas_call(lambda *refs: expert_kernel(width, *refs), out_shape=jax.S...  7.84 us
    pallas_call x1, Pallas kernels, per_device(): pl.pallas_call(lambda *refs: combine_kernel(dims, *refs), out_shape=jax.S...  4.55 us
  transfers between devices with their start and end apart: 2, of which 2 were waited for; matrix products, arithmetic and copies ran while one was open for 0% of the time, Pallas kernels for 0%

profile of v2, /device:TPU:1, one launch (start us, length us, event | category | flops | bytes accessed | tf_op | source)
XLA Modules:
  0.0 215.8 jit_solution(11929472372239260367)
XLA Ops:
  7.2 0.0 all-gather.2.cloned.1.call-start
  7.2 0.7 reduce_precision.6
  7.9 0.8 copy.14
  8.7 0.7 convert_element_type.15
  9.3 0.1 copy.16
  9.4 0.1 copy.13
  9.5 1.6 concatenate.3
  11.1 0.0 all-gather.2.cloned.1.call-update
  11.1 0.0 reduce-scatter.2.cloned.1.call-start
  11.2 62.4 %all-gather.2.cloned.1.call-done.refs_1_ = bf16[128,4224]{1,0:T(8,128)(2,1)} async-done(((bf16[16,4224]{1,0:T(8,128)(2,1)}), bf16[128,4224]{1,0:T(8,128)(2,1)}) %all-gather.2.cloned.1.call-update) | async-done | bytes 1081360 | tf_op jit(solution)/shard_map/all_gather | solution.py:154
  73.6 3.9 %dispatch.1 = (bf16[256,4096]{1,0:T(8,128)(2,1)}, bf16[128,256]{1,0:T(8,128)(2,1)}, bf16[128,256]{1,0:T(8,128)(2,1)}, bf16[128,256]{1,0:T(8,128)(2,1)}) custom-call(s32[1]{0:T(128)} %bitcast.refs_0_, bf16[128,4224]{1,0:T(8,128)(2,1)} %all-gather.2.cloned.1.call-done.refs_1_), custom_call_target="tpu_custom_call" | custom-call | tf_op jit(solution)/shard_map/dispatch/pallas_call | solution.py:157
  77.5 35.1 %all_to_all.10 = bf16[16,16,4096]{2,1,0:T(8,128)(2,1)} all-to-all(bf16[16,16,4096]{2,1,0:T(8,128)(2,1)} %bitcast.11), channel_id=1, replica_groups={{0,1,2,3,4,5,6,7,8,9,10,11,12,13,14,15},{16,17,18,19,20,21,22,23,24,25,..., dimensions={0} | all-to-all | bytes 4194304 | tf_op jit(solution)/shard_map/all_to_all | solution.py:171
  112.6 7.8 %expert.1 = bf16[256,4096]{1,0:T(8,128)(2,1)} custom-call(bf16[256,4096]{1,0:T(8,128)(2,1)} %bitcast.7, bf16[2048,768]{1,0:T(8,128)(2,1)} %bitcast.10, bf16[384,2048]{1,0:T(8,128)(2,1)} %bitcast.12), custom_call_target="tpu_custom_call" | custom-call | tf_op jit(solution)/shard_map/expert/pallas_call | solution.py:181
  120.4 32.1 %all_to_all.11 = bf16[16,16,4096]{2,1,0:T(8,128)(2,1)} all-to-all(bf16[16,16,4096]{2,1,0:T(8,128)(2,1)} %bitcast.8), channel_id=1, replica_groups={{0,1,2,3,4,5,6,7,8,9,10,11,12,13,14,15},{16,17,18,19,20,21,22,23,24,25,..., dimensions={0} | all-to-all | bytes 4194304 | tf_op jit(solution)/shard_map/all_to_all | solution.py:171
  152.5 4.5 %combine.1 = bf16[128,4224]{1,0:T(8,128)(2,1)} custom-call(s32[1]{0:T(128)} %bitcast.refs_0_, bf16[128,4224]{1,0:T(8,128)(2,1)} %all-gather.2.cloned.1.call-done.refs_1_, bf16[256,4096]{1,0:T(8,128)(2,1)} %bitcast.9, bf16[128,256]{1,0:T(8,128)(2,1)} %get-tuple-element.8.refs_3_, bf16[128,256]{1,0:T(8,128)(2,1)} %get-tuple-element.9.refs_4_, ...), custom_call_target="tpu_custom_call" | custom-call | tf_op jit(solution)/shard_map/combine/pallas_call | solution.py:189
  157.1 0.0 reduce-scatter.2.cloned.1.call-update
  157.1 48.9 %reduce-scatter.2.cloned.1.call-done = bf16[16,4224]{1,0:T(8,128)(2,1)} async-done(((bf16[128,4224]{1,0:T(8,128)(2,1)}), bf16[16,4224]{1,0:T(8,128)(2,1)}) %reduce-scatter.2.cloned.1.call-update) | async-done | bytes 135184 | tf_op jit(solution)/shard_map/reduce_scatter | solution.py:196
  206.0 0.7 slice_convert_fusion
  206.7 0.1 slice_add_fusion
  206.7 0.7 copy.17
  207.4 1.5 fusion.1
  (2 shorter events, 0.0 us)
Async XLA Ops:
  7.2 66.4 %all-gather.2.cloned.1.call-start = ((), (), s32[]{:S(2)}) async-start(), calls=%async_computation.3 | async-start | bytes 1216512 | tf_op jit(solution)/shard_map/all_gather | solution.py:154
  11.1 194.8 %reduce-scatter.2.cloned.1.call-start = ((), (), s32[]{:S(2)}) async-start(), calls=%async_computation.4 | async-start | bytes 1216512 | tf_op jit(solution)/shard_map/reduce_scatter | solution.py:196
Sparse Core Ops, SparseCore 0:
  11.3 62.2 all-gather.1
  157.2 48.7 reduce-scatter.1

commit v3 on v2

--- a/solution.py
+++ b/solution.py
@@ -7,6 +7,7 @@
 
 EXTRA = 128
 PAIR = 2
+SMALL = 20 << 20
 F32 = jnp.float32
 BF16 = jnp.bfloat16
 
@@ -123,6 +124,36 @@
     ).astype(BF16)
 
 
+def pack_kernel(tokens_ref, cotangent_ref, ids_ref, combine_ref, out_ref):
+    top = ids_ref.shape[0]
+    width = tokens_ref.shape[1]
+    out_ref[:, :width] = tokens_ref[...]
+    out_ref[:, width : 2 * width] = cotangent_ref[...]
+    ids = ids_ref[...].astype(F32).astype(BF16)
+    row = lax.broadcasted_iota(jnp.int32, (top, EXTRA), 0)
+    lane = lax.broadcasted_iota(jnp.int32, (top, EXTRA), 1)
+    info = jnp.zeros((out_ref.shape[0], EXTRA), F32)
+    for i, piece in enumerate((ids,) + split3(combine_ref[...])):
+        spread = jnp.where(lane == row + i * top, 1.0, 0.0).astype(BF16)
+        info = info + lax.dot_general(
+            piece, spread, (((0,), (0,)), ((), ())), preferred_element_type=F32
+        )
+    out_ref[:, 2 * width :] = info.astype(BF16)
+
+
+def unpack_kernel(sum_ref, mixed_ref, grad_ref, weights_ref):
+    top = weights_ref.shape[0]
+    width = mixed_ref.shape[1]
+    mixed_ref[...] = sum_ref[:, :width]
+    grad_ref[...] = sum_ref[:, width : 2 * width]
+    row = lax.broadcasted_iota(jnp.int32, (top, EXTRA), 0)
+    lane = lax.broadcasted_iota(jnp.int32, (top, EXTRA), 1)
+    fold = jnp.where((lane % top == row) & (lane < 3 * top), 1.0, 0.0).astype(BF16)
+    weights_ref[...] = lax.dot_general(
+        fold, sum_ref[:, 2 * width :], (((1,), (1,)), ((), ())), preferred_element_type=F32
+    )
+
+
 def per_device(tokens, cotangent, expert_ids, combine, w_gate_up, w_down):
     nodes = lax.axis_size("node")
     locals_ = lax.axis_size("local")
@@ -137,23 +168,16 @@
     slots = peers * blocks * cap
     count = blocks * rows
     node = (lax.axis_index("node") // PAIR).astype(jnp.int32).reshape(1)
-    hi = lax.reduce_precision(combine, 8, 7)
-    mid = lax.reduce_precision(combine - hi, 8, 7)
-    low = combine - hi - mid
-    pieces = (hi.astype(BF16), mid.astype(BF16), low.astype(BF16))
-    packed = jnp.concatenate(
-        [
-            tokens,
-            cotangent,
-            expert_ids.astype(BF16),
-            *pieces,
-            jnp.zeros((rows, EXTRA - 4 * top), BF16),
-        ],
-        axis=1,
-    )
-    gathered = lax.all_gather(packed, "node", axis_index_groups=rings, axis=0, tiled=True)
     smem = pl.BlockSpec(memory_space=pltpu.SMEM)
     vmem = pl.BlockSpec(memory_space=pltpu.VMEM)
+    packed = pl.pallas_call(
+        pack_kernel,
+        out_shape=jax.ShapeDtypeStruct((rows, 2 * width + EXTRA), BF16),
+        in_specs=[vmem] * 4,
+        out_specs=vmem,
+        name="pack",
+    )(tokens, cotangent, expert_ids.T, combine.T)
+    gathered = lax.all_gather(packed, "node", axis_index_groups=rings, axis=0, tiled=True)
     send, place, hi, mid = pl.pallas_call(
         lambda *refs: dispatch_kernel(dims, *refs),
         out_shape=(
@@ -164,6 +188,7 @@
         ),
         in_specs=[smem, vmem],
         out_specs=(vmem,) * 4,
+        compiler_params=pltpu.CompilerParams(vmem_limit_bytes=SMALL),
         name="dispatch",
     )(node, gathered)
 
@@ -183,6 +208,7 @@
         out_shape=jax.ShapeDtypeStruct((slots, 2 * width), BF16),
         in_specs=[vmem] * 3,
         out_specs=vmem,
+        compiler_params=pltpu.CompilerParams(vmem_limit_bytes=SMALL),
         name="expert",
     )(arrived.reshape(slots, 2 * width), w_gate_up[0], w_down[0])
     returned = exchange(worked)
@@ -191,14 +217,24 @@
         out_shape=jax.ShapeDtypeStruct((count, 2 * width + EXTRA), BF16),
         in_specs=[smem] + [vmem] * 5,
         out_specs=vmem,
+        compiler_params=pltpu.CompilerParams(vmem_limit_bytes=SMALL),
         name="combine",
     )(node, gathered, returned.reshape(slots, 2 * width), place, hi, mid)
     summed = lax.psum_scatter(
         partial, "node", scatter_dimension=0, axis_index_groups=rings, tiled=True
     )
-    last = summed[:, 2 * width :].astype(F32)
-    grad_combine = last[:, :top] + last[:, top : 2 * top] + last[:, 2 * top : 3 * top]
-    return summed[:, :width], summed[:, width : 2 * width], grad_combine
+    mixed, grad_tokens, grad_combine = pl.pallas_call(
+        unpack_kernel,
+        out_shape=(
+            jax.ShapeDtypeStruct((rows, width), BF16),
+            jax.ShapeDtypeStruct((rows, width), BF16),
+            jax.ShapeDtypeStruct((top, rows), F32),
+        ),
+        in_specs=[vmem],
+        out_specs=(vmem,) * 3,
+        name="unpack",
+    )(summed)
+    return mixed, grad_tokens, grad_combine.T
 
 
 def solution(mesh):

time: 219 us -> 207 us (0.945)
  Pallas kernels: 16.3 us -> 10.8 us
  local copies, waits for them, and re-layouts: 4.71 us -> 1.25 us
    pallas_call x1, Pallas kernels: 7.84 us -> 3.53 us  [per_device(): pl.pallas_call(lambda *refs: expert_kernel(width, *refs), out_shape=jax.S...]
    pallas_call x0 -> x2, Pallas kernels: none -> 3.31 us  [the longest x1 1.69 us: per_device(): pl.pallas_call(pack_kernel, out_shape=jax.ShapeDtypeStruct((rows, 2 * wid...]
    pallas_call x1, Pallas kernels: 3.88 us -> 1.28 us  [per_device(): pl.pallas_call(lambda *refs: dispatch_kernel(dims, *refs), out_shape=(jax...]
where the time goes in v3:
time: 207 us; the launch traced here: 204 us
  waiting for transfers between devices  113 us (55%)
  blocking collectives  65.5 us (32%)
  between operations  14.1 us (7%)
  Pallas kernels  10.8 us (5%)
    all_to_all x2, blocking collectives, exchange(): lax.all_to_all(value.reshape(peers, blocks * cap, 2 * width), ('node', 'l...  65.5 us
    all_gather x1, waiting for transfers between devices, per_device(): lax.all_gather(packed, 'node', axis_index_groups=rings, axis=0, tiled=True)  64 us
    reduce_scatter x1, waiting for transfers between devices, per_device(): lax.psum_scatter(partial, 'node', scatter_dimension=0, axis_index_groups=...  48.7 us
  transfers between devices with their start and end apart: 2, of which 2 were waited for; matrix products, arithmetic and copies ran while one was open for 0% of the time, Pallas kernels for 0%

profile of v3, /device:TPU:1, one launch (start us, length us, event | category | flops | bytes accessed | tf_op | source)
XLA Modules:
  0.0 204.4 jit_solution(2839810183749779968)
XLA Ops:
  7.2 0.0 all-gather.2.cloned.1.call-start
  7.2 1.7 pack.1
  8.9 0.0 all-gather.2.cloned.1.call-update
  8.9 0.0 reduce-scatter.2.cloned.1.call-start
  9.0 64.0 %all-gather.2.cloned.1.call-done.refs_1_ = bf16[128,4224]{1,0:T(8,128)(2,1)} async-done(((bf16[16,4224]{1,0:T(8,128)(2,1)}), bf16[128,4224]{1,0:T(8,128)(2,1)}) %all-gather.2.cloned.1.call-update) | async-done | bytes 1081360 | tf_op jit(solution)/shard_map/all_gather | solution.py:180
  72.9 0.0 copy-start
  72.9 1.2 copy-done
  74.2 0.0 copy-start.3
  74.2 1.3 dispatch.1
  75.5 0.0 copy-start.2
  75.5 35.1 %all_to_all.10 = bf16[16,16,4096]{2,1,0:T(8,128)(2,1)S(1)} all-to-all(bf16[16,16,4096]{2,1,0:T(8,128)(2,1)S(1)} %bitcast.14), channel_id=1, replica_groups={{0,1,2,3,4,5,6,7,8,9,10,11,12,13,14,15},{16,17,18,19,20,21,22,23,24,25,..., dimensions={0} | all-to-all | bytes 4194304 | tf_op jit(solution)/shard_map/all_to_all | solution.py:196
  110.6 0.0 copy-done.3
  110.6 0.0 copy-done.2
  110.6 3.5 %expert.1 = bf16[256,4096]{1,0:T(8,128)(2,1)S(1)} custom-call(bf16[256,4096]{1,0:T(8,128)(2,1)S(1)} %bitcast.10, bf16[2048,768]{1,0:T(8,128)(2,1)S(1)} %bitcast.13, bf16[384,2048]{1,0:T(8,128)(2,1)S(1)} %bitcast.15), custom_call_target="tpu_custom_call" | custom-call | tf_op jit(solution)/shard_map/expert/pallas_call | solution.py:206
  114.1 0.0 copy-start.1
  114.1 30.5 %all_to_all.11 = bf16[16,16,4096]{2,1,0:T(8,128)(2,1)S(1)} all-to-all(bf16[16,16,4096]{2,1,0:T(8,128)(2,1)S(1)} %bitcast.11), channel_id=1, replica_groups={{0,1,2,3,4,5,6,7,8,9,10,11,12,13,14,15},{16,17,18,19,20,21,22,23,24,25,..., dimensions={0} | all-to-all | bytes 4194304 | tf_op jit(solution)/shard_map/all_to_all | solution.py:196
  144.6 0.0 copy-done.1
  144.6 2.6 %combine.1 = bf16[128,4224]{1,0:T(8,128)(2,1)} custom-call(s32[1]{0:T(128)} %bitcast.refs_0_, bf16[128,4224]{1,0:T(8,128)(2,1)S(1)} %copy-done.1, bf16[256,4096]{1,0:T(8,128)(2,1)S(1)} %bitcast.12, bf16[128,256]{1,0:T(8,128)(2,1)S(1)} %get-tuple-element.11.refs_3_, bf16[128,256]{1,0:T(8,128)(2,1)S(1)} %get-tuple-element.12.refs_4_, ...), custom_call_target="tpu_custom_call" | custom-call | tf_op jit(solution)/shard_map/combine/pallas_call | solution.py:215
  147.2 0.0 reduce-scatter.2.cloned.1.call-update
  147.2 48.7 %reduce-scatter.2.cloned.1.call-done.sum_ref = bf16[16,4224]{1,0:T(8,128)(2,1)} async-done(((bf16[128,4224]{1,0:T(8,128)(2,1)}), bf16[16,4224]{1,0:T(8,128)(2,1)}) %reduce-scatter.2.cloned.1.call-update) | async-done | bytes 135184 | tf_op jit(solution)/shard_map/reduce_scatter | solution.py:223
  195.9 1.6 unpack.1
Async XLA Ops:
  7.2 65.8 %all-gather.2.cloned.1.call-start = ((), (), s32[]{:S(2)}) async-start(), calls=%async_computation.3 | async-start | bytes 1216512 | tf_op jit(solution)/shard_map/all_gather | solution.py:180
  8.9 187.0 %reduce-scatter.2.cloned.1.call-start = ((), (), s32[]{:S(2)}) async-start(), calls=%async_computation.4 | async-start | bytes 1216512 | tf_op jit(solution)/shard_map/reduce_scatter | solution.py:223
  72.9 1.2 copy-start
  74.2 36.4 %copy-start.3 = (bf16[1,384,2048]{2,1,0:T(8,128)(2,1)S(1)}, bf16[1,384,2048]{2,1,0:T(8,128)(2,1)}, u32[]{:S(2)}) copy-start(bf16[1,384,2048]{2,1,0:T(8,128)(2,1)} %param.11) | copy-start | bytes 4718596
  75.5 35.1 %copy-start.2 = (bf16[1,2048,768]{2,1,0:T(8,128)(2,1)S(1)}, bf16[1,2048,768]{2,1,0:T(8,128)(2,1)}, u32[]{:S(2)}) copy-start(bf16[1,2048,768]{2,1,0:T(8,128)(2,1)} %param.10) | copy-start | bytes 9437188
  114.1 30.5 %copy-start.1 = (bf16[128,4224]{1,0:T(8,128)(2,1)S(1)}, bf16[128,4224]{1,0:T(8,128)(2,1)}, u32[]{:S(2)}) copy-start(bf16[128,4224]{1,0:T(8,128)(2,1)} %all-gather.2.cloned.1.call-done.refs_1_) | copy-start | bytes 3244036
Sparse Core Ops, SparseCore 0:
  10.6 62.2 all-gather.1
  147.4 48.5 reduce-scatter.1
